TPU v7x, 32 devices: a whole 2x2x4 slice. The times are simulated.
32 devices in a mesh: row: 8 (over z, x), col: 2 (over core), rank: 2 (over y).
Axes of the slice: x: 2, y: 2, z: 4, core: 2. Of those that a mesh axis runs over, the one named last changes fastest.
Arguments:
- tensor: bfloat16 [64, 2048, 2048], P(None, 'row', 'col'), may hold values from -6 to 6
- aux_factor: bfloat16 [64, 256], P(None, 'rank'), may hold values from -0.75 to 0.75
- row_factor: bfloat16 [2048, 256], P(('row', 'col'), 'rank'), may hold values from -0.125 to 0.125
- col_factor: bfloat16 [2048, 256], P(('col', 'row'), 'rank'), may hold values from -0.125 to 0.125
Outputs:
- row_result: float32 [2048, 256], P(('row', 'col'), 'rank')
- aux_result: float32 [64, 256], P('row', 'rank')
All inputs are finite; a program needn't handle non-finite values.
Results may differ from a plain program's by a relative error of at most 0.0003.
Values may be sent and summed in bfloat16 or wider, within the bound.
A program may use at most 128 MiB of HBM per device.

v0:
```python
import jax
import jax.numpy as jnp
from jax import lax
from jax.sharding import PartitionSpec as P


def reduce_inner(inner, aux_factor, row_panel):
    aux_panel = aux_factor.astype(jnp.float32)
    aux_count = inner.shape[0]
    row_total = jnp.zeros((inner.shape[1], inner.shape[2]), jnp.float32)
    pieces = []
    for start in range(0, aux_count, 8):
        block = inner[start : start + 8]
        row_total = row_total + jnp.sum(block * aux_panel[start : start + 8][:, None, :], axis=0)
        pieces.append(jnp.sum(block * row_panel[None, :, :], axis=1))
    return (row_total, jnp.concatenate(pieces, axis=0))


def body(tensor, aux_factor, row_factor, col_factor):
    row_panel = lax.all_gather(row_factor, "col", axis=0, tiled=True).astype(jnp.float32)
    width = aux_factor.shape[1]
    aux_count = tensor.shape[0]
    orbits = tensor.shape[1]
    flat = tensor.reshape(aux_count * orbits, tensor.shape[2])
    columns = lax.all_gather(col_factor, "row", axis=0, tiled=True)
    inner = jnp.dot(flat, columns, preferred_element_type=jnp.float32)
    inner = inner.reshape(aux_count, orbits, width)
    row_total, aux_total = reduce_inner(inner, aux_factor, row_panel)
    row_result = lax.psum_scatter(row_total, "col", scatter_dimension=0, tiled=True)
    scattered = lax.psum_scatter(aux_total, "row", scatter_dimension=0, tiled=True)
    aux_result = lax.psum(scattered, "col")
    return (row_result, aux_result)


def solution(mesh):
    return jax.shard_map(
        body,
        mesh=mesh,
        in_specs=(
            P(None, "row", "col"),
            P(None, "rank"),
            P(("row", "col"), "rank"),
            P(("col", "row"), "rank"),
        ),
        out_specs=(P(("row", "col"), "rank"), P("row", "rank")),
        check_vma=False,
    )
```

profile of v0, /device:TPU:0, one launch (start us, length us, event | category | flops | bytes accessed | tf_op | source)
XLA Modules:
  0.0 115.6 jit_solution(7216242594102125668)
XLA Ops:
  7.2 0.0 reduce-scatter.2.cloned.1.call-start
  7.2 0.8 fusion.1
  8.0 32.8 %all_gather.6 = bf16[1024,128]{1,0:T(8,128)(2,1)S(1)} all-gather(bf16[128,128]{1,0:T(8,128)(2,1)} %param.7), channel_id=1, replica_groups=mesh['row'=8,'col'=2,'rank'=2] {'row'}, dimensions={0}, use_global_device_ids=true | all-gather | bytes 294912 | tf_op jit(solution)/shard_map/all_gather | solution.py:25
  40.8 0.0 copy-start.1
  40.8 0.0 copy-start.2
  40.8 14.9 %fusion.2 = f32[16384,128]{1,0:T(8,128)S(1)} fusion(bf16[16384,1024]{1,0:T(8,128)(2,1)} %bitcast.20, bf16[1024,128]{1,0:T(8,128)(2,1)S(1)} %all_gather.6), kind=kOutput, calls=%fused_computation.28 | convolution fusion | flops 4294967296 | bytes 42205184 | tf_op jit(solution)/shard_map/dot_general | solution.py:26
  55.7 0.0 copy-start
  55.7 3.2 %copy-done = f32[16384,128]{1,0:T(8,128)} copy-done((f32[16384,128]{1,0:T(8,128)}, f32[16384,128]{1,0:T(8,128)S(1)}, u32[]{:S(2)}) %copy-start) | copy-done | bytes 8388632
  58.9 0.6 fusion
  59.5 0.2 multiply_reduce_fusion.14
  59.6 0.2 multiply_reduce_fusion.8
  59.8 0.2 multiply_reduce_fusion.10
  59.9 0.2 multiply_reduce_fusion.12
  60.1 0.7 add_add_fusion
  60.8 0.0 reduce-scatter.2.cloned.1.call-update
  60.8 0.0 copy-done.1
  60.8 1.9 %all_gather.7 = bf16[256,128]{1,0:T(8,128)(2,1)S(1)} all-gather(bf16[128,128]{1,0:T(8,128)(2,1)S(1)} %copy-done.1), channel_id=1, replica_groups=mesh['row'=8,'col'=2,'rank'=2] {'col'}, dimensions={0}, use_global_device_ids=true | all-gather | bytes 98304 | tf_op jit(solution)/shard_map/all_gather | solution.py:20
  62.7 4.6 %multiply_reduce_fusion = (f32[8,128]{1,0:T(8,128)S(1)}, f32[8,128]{1,0:T(8,128)S(1)}, f32[8,128]{1,0:T(8,128)S(1)}, f32[8,128]{1,0:T(8,128)S(1)}, f32[8,128]{1,...) fusion(f32[256,128]{1,0:T(8,128)S(1)} %convert_element_type.7, f32[16384,128]{1,0:T(8,128)} %copy-done), kind=kLoop, calls=%fused_computation | loop fusion | flops 4186112 | bytes 8552448 | tf_op jit(solution)/shard_map/reduce_sum | solution.py:15
  67.4 0.0 copy-done.2
  67.4 0.6 dynamic-slice
  68.6 37.1 %all-reduce = f32[64,128]{1,0:T(8,128)S(1)} all-reduce(f32[64,128]{1,0:T(8,128)S(1)} %constant_dynamic-update-slice_fusion), channel_id=3, replica_groups=mesh['row'=8,'col'=2,'rank'=2] {'row'}, use_global_device_ids=true, to_apply=%region_17.0.clone | all-reduce | flops 8192 | bytes 65536
  105.7 3.0 %psum.7 = f32[8,128]{1,0:T(8,128)} all-reduce(f32[8,128]{1,0:T(8,128)S(1)} %constant_dynamic-slice_fusion), channel_id=1, replica_groups=mesh['row'=8,'col'=2,'rank'=2] {'col'}, use_global_device_ids=true, to_apply=%region_18.0 | all-reduce | flops 1024 | bytes 8192 | tf_op jit(solution)/shard_map/psum | solution.py:31
  108.8 0.0 reduce-scatter.2.cloned.1.call-done
  (10 shorter events, 0.0 us)
Async XLA Ops:
  7.2 101.6 %reduce-scatter.2.cloned.1.call-start = ((), (), s32[]{:S(2)}) async-start(), calls=%async_computation.1 | async-start | bytes 196608 | tf_op jit(solution)/shard_map/reduce_scatter | solution.py:29
  40.8 20.1 %copy-start.1 = (bf16[128,128]{1,0:T(8,128)(2,1)S(1)}, bf16[128,128]{1,0:T(8,128)(2,1)}, u32[]{:S(2)}) copy-start(bf16[128,128]{1,0:T(8,128)(2,1)} %param.6) | copy-start | bytes 98308
  40.8 26.6 %copy-start.2 = (u32[32]{0:T(128)S(1)}, u32[32]{0:T(128)}, u32[]{:S(2)}) copy-start(u32[32]{0:T(128)} %constant.4) | copy-start | bytes 388
  55.7 3.2 %copy-start = (f32[16384,128]{1,0:T(8,128)}, f32[16384,128]{1,0:T(8,128)S(1)}, u32[]{:S(2)}) copy-start(f32[16384,128]{1,0:T(8,128)S(1)} %fusion.2) | copy-start | bytes 25165828
Sparse Core Ops, SparseCore 0:
  61.0 8.5 reduce-scatter.1
where the time goes:
time: 116 us
  blocking collectives  74.7 us (64%)
  matrix products  14.9 us (13%)
  between operations  14.8 us (13%)
  other arithmetic  5.94 us (5%)
  local copies, waits for them, and re-layouts  5.2 us (4%)
    unnamed x1, blocking collectives  37.1 us
    all_gather x1, blocking collectives, body(): columns = lax.all_gather(col_factor, 'row', axis=0, tiled=True)  32.8 us
    dot_general x1, matrix products, body(): inner = jnp.dot(flat, columns, preferred_element_type=jnp.float32)  14.9 us
    reduce_sum x1, other arithmetic, reduce_inner(): pieces.append(jnp.sum(block * row_panel[None, :, :], axis=1))  4.59 us
    unnamed x15, local copies, waits for them, and re-layouts  3.83 us
    psum x1, blocking collectives, body(): aux_result = lax.psum(scattered, 'col')  3.04 us
  transfers between devices with their start and end apart: 1, of which 0 were waited for; matrix products, arithmetic and copies ran while one was open for 5% of the time, Pallas kernels for 0%

commit v1 on v0

--- a/solution.py
+++ b/solution.py
@@ -1,7 +1,36 @@
+import functools
 import jax
 import jax.numpy as jnp
 from jax import lax
 from jax.sharding import PartitionSpec as P
+
+
+def render_marks_on_mesh(x_part, dim_no):
+    x_part = jnp.moveaxis(x_part, 0, dim_no)
+    tile_out = x_part.shape
+    return x_part.reshape(
+        *tile_out[:dim_no], tile_out[dim_no] * tile_out[dim_no + 1], *tile_out[dim_no + 2 :]
+    )
+
+
+def _point_sides(target, axis_name):
+    wide_n = lax.psum(1, axis_name=axis_name)
+    taken_in = target[None]
+    for k in range(wide_n.bit_length() - 1):
+        carry = 1 << k
+        val2 = lax.ppermute(taken_in, axis_name, [(rr, rr ^ carry) for rr in range(wide_n)])
+        e_next = jnp.stack([taken_in, val2])
+        even = lax.axis_index(axis_name) >> k & 1
+        taken_in = jnp.where(even == 0, e_next, e_next[::-1]).reshape(-1, *target.shape)
+    return taken_in
+
+
+def sections_touch(shard_in, local_values, at_axis):
+    top = _point_sides(shard_in, local_values)
+    return render_marks_on_mesh(top, at_axis)
+
+
+shape_pairs_all_on_mesh = functools.partial(sections_touch, local_values="row", at_axis=0)
 
 
 def reduce_inner(inner, aux_factor, row_panel):
@@ -22,7 +51,7 @@
     aux_count = tensor.shape[0]
     orbits = tensor.shape[1]
     flat = tensor.reshape(aux_count * orbits, tensor.shape[2])
-    columns = lax.all_gather(col_factor, "row", axis=0, tiled=True)
+    columns = shape_pairs_all_on_mesh(col_factor)
     inner = jnp.dot(flat, columns, preferred_element_type=jnp.float32)
     inner = inner.reshape(aux_count, orbits, width)
     row_total, aux_total = reduce_inner(inner, aux_factor, row_panel)

time: 116 us -> 110 us (0.948)
  blocking collectives: 74.7 us -> 41.5 us
  local copies, waits for them, and re-layouts: 5.2 us -> 15 us
  starting transfers between devices: 0.04 us -> 8.34 us
  matrix products: 14.9 us -> 19 us
  other arithmetic: 5.94 us -> 8.59 us
  waiting for transfers between devices: 0.02 us -> 2.22 us
    all_gather x1 -> x0, blocking collectives: 32.8 us -> none  [body(): columns = lax.all_gather(col_factor, 'row', axis=0, tiled=True)]
    ppermute x0 -> x3, starting transfers between devices: none -> 8.3 us  [_point_sides(): lax.ppermute(taken_in, axis_name, [(rr, rr ^ carry) for rr in range(wide_...]
    dot_general x1, matrix products: 14.9 us -> 19 us  [body(): inner = jnp.dot(flat, columns, preferred_element_type=jnp.float32)]
    slice x1, local copies, waits for them, and re-layouts: 0.57 us -> 3.99 us  [reduce_inner(): block = inner[start:start + 8]]
    slice x1 -> x9, local copies, waits for them, and re-layouts: 0.8 us -> 4.09 us  [reduce_inner(): aux_panel[start:start + 8][:, None, :]]
    ppermute x0 -> x3, waiting for transfers between devices: none -> 2.2 us  [_point_sides(): lax.ppermute(taken_in, axis_name, [(rr, rr ^ carry) for rr in range(wide_...]
    reduce_sum x4, other arithmetic: 0.64 us -> 2.6 us  [reduce_inner(): jnp.sum(block * aux_panel[start:start + 8][:, None, :], axis=0)]
    unnamed x15 -> x29, local copies, waits for them, and re-layouts: 3.83 us -> 5.58 us
  transfers between devices with their start and end apart: 1 -> 4, of which waited for: 0 -> 2; matrix products, arithmetic and copies ran while one was open for 5% -> 10% of each run, Pallas kernels for 0% -> 0%
where the time goes in v1:
time: 110 us
  blocking collectives  41.5 us (38%)
  matrix products  19 us (17%)
  local copies, waits for them, and re-layouts  15 us (14%)
  between operations  15 us (14%)
  other arithmetic  8.59 us (8%)
  starting transfers between devices  8.34 us (8%)
  waiting for transfers between devices  2.22 us (2%)
    unnamed x1, blocking collectives  36.4 us
    dot_general x1, matrix products, body(): inner = jnp.dot(flat, columns, preferred_element_type=jnp.float32)  19 us
    ppermute x3, starting transfers between devices, _point_sides(): lax.ppermute(taken_in, axis_name, [(rr, rr ^ carry) for rr in range(wide_...  8.3 us
    unnamed x29, local copies, waits for them, and re-layouts  5.58 us
    reduce_sum x1, other arithmetic, reduce_inner(): pieces.append(jnp.sum(block * row_panel[None, :, :], axis=1))  4.36 us
    slice x9, local copies, waits for them, and re-layouts, reduce_inner(): aux_panel[start:start + 8][:, None, :]  4.09 us
    slice x1, local copies, waits for them, and re-layouts, reduce_inner(): block = inner[start:start + 8]  3.99 us
    psum x1, blocking collectives, body(): aux_result = lax.psum(scattered, 'col')  3.04 us
  transfers between devices with their start and end apart: 4, of which 2 were waited for; matrix products, arithmetic and copies ran while one was open for 10% of the time, Pallas kernels for 0%

profile of v1, /device:TPU:0, one launch (start us, length us, event | category | flops | bytes accessed | tf_op | source)
XLA Modules:
  0.0 109.6 jit_solution(4599304864939741165)
XLA Ops:
  7.2 3.0 %collective-permute-start = (bf16[1,128,128]{2,1,0:T(8,128)(2,1)}, bf16[1,128,128]{2,1,0:T(8,128)(2,1)S(1)}, u32[]{:S(2)}, u32[]{:S(2)}) collective-permute-start(bf16[1,128,128]{2,1,0:T(8,128)(2,1)} %bitcast.80), channel_id=1, source_target_pairs={{0,4},{4,0},{8,12},{12,8},{16,20},{20,16},{24,28},{28,24},{1,5},{5... | collective-permute-start | bytes 98312 | tf_op jit(solution)/shard_map/ppermute | solution.py:21
  10.2 2.1 %collective-permute-done = bf16[1,128,128]{2,1,0:T(8,128)(2,1)S(1)} collective-permute-done((bf16[1,128,128]{2,1,0:T(8,128)(2,1)}, bf16[1,128,128]{2,1,0:T(8,128)(2,1)S(1)}, u32[]{:S(2)}, u32[]{:S(2)}) %collective-permute-start) | collective-permute-done | bytes 32800 | tf_op jit(solution)/shard_map/ppermute | solution.py:21
  12.3 0.8 pad_maximum_fusion.2
  13.1 2.2 %collective-permute-start.1 = (bf16[2,128,128]{2,1,0:T(8,128)(2,1)S(1)}, bf16[2,128,128]{2,1,0:T(8,128)(2,1)S(1)}, u32[]{:S(2)}, u32[]{:S(2)}) collective-permute-start(bf16[2,128,128]{2,1,0:T(8,128)(2,1)S(1)} %get-tuple-element.21), channel_id=1, source_target_pairs={{0,8},{4,12},{8,0},{12,4},{16,24},{20,28},{24,16},{28,20},{1,9},{5... | collective-permute-start | bytes 196616 | tf_op jit(solution)/shard_map/ppermute | solution.py:21
  15.3 2.1 %all_gather.3 = bf16[256,128]{1,0:T(8,128)(2,1)S(1)} all-gather(bf16[128,128]{1,0:T(8,128)(2,1)} %param.6), channel_id=1, replica_groups=mesh['row'=8,'col'=2,'rank'=2] {'col'}, dimensions={0}, use_global_device_ids=true | all-gather | bytes 98304 | tf_op jit(solution)/shard_map/all_gather | solution.py:49
  17.6 3.1 %collective-permute-start.2 = (bf16[4,128,128]{2,1,0:T(8,128)(2,1)S(1)}, bf16[4,128,128]{2,1,0:T(8,128)(2,1)S(1)}, u32[]{:S(2)}, u32[]{:S(2)}) collective-permute-start(bf16[4,128,128]{2,1,0:T(8,128)(2,1)S(1)} %bitcast.76), channel_id=1, source_target_pairs={{0,16},{4,20},{8,24},{12,28},{16,0},{20,4},{24,8},{28,12},{1,17},{... | collective-permute-start | bytes 393224 | tf_op jit(solution)/shard_map/ppermute | solution.py:21
  20.7 0.8 fusion.3
  21.5 0.7 copy.15
  22.2 0.7 copy.16
  23.0 0.7 copy.18
  24.1 0.7 copy.22
  24.8 1.2 %dynamic-slice = u32[1]{0:T(128)} dynamic-slice(u32[32]{0:T(128)} %constant.16, u32[]{:T(128)S(6)} %add.35), dynamic_slice_sizes={1} | dynamic-slice | bytes 12
  26.9 19.0 %convolution_bitcast_fusion = f32[16384,128]{0,1:T(8,128)} fusion(bf16[1024,128]{1,0:T(8,128)(2,1)S(1)} %bitcast.75, bf16[16384,1024]{1,0:T(8,128)(2,1)} %bitcast.58), kind=kOutput, calls=%fused_computation | convolution fusion | flops 4294967296 | bytes 42205184 | tf_op jit(solution)/shard_map/dot_general | solution.py:55
  45.9 4.0 %fusion.2 = (f32[2048,128]{0,1:T(8,128)S(1)}, f32[2048,128]{0,1:T(8,128)S(1)}, f32[2048,128]{0,1:T(8,128)S(1)}, f32[2048,128]{0,1:T(8,128)S(1)}, f32[2048,128]{0...) fusion(f32[16384,128]{0,1:T(8,128)} %convolution_bitcast_fusion), kind=kLoop, calls=%fused_computation.27 | loop fusion | bytes 16777216 | tf_op jit(solution)/shard_map/slice | solution.py:42
  49.9 0.3 copy.26
  50.2 0.3 copy.27
  50.6 0.3 copy.28
  50.9 0.3 copy.29
  51.3 0.3 copy.30
  51.6 0.3 copy.31
  52.0 0.3 copy.32
  52.4 0.3 copy.33
  52.7 0.7 multiply_reduce_fusion.14
  53.4 0.7 multiply_reduce_fusion.12
  54.1 0.6 multiply_reduce_fusion.10
  54.8 0.6 multiply_reduce_fusion.8
  55.4 0.7 add_add_fusion
  56.2 4.4 %multiply_reduce_fusion = (f32[8,128]{0,1:T(8,128)S(1)}, f32[8,128]{0,1:T(8,128)S(1)}, f32[8,128]{0,1:T(8,128)S(1)}, f32[8,128]{0,1:T(8,128)S(1)}, f32[8,128]{0,...) fusion(f32[8,256,128]{1,0,2:T(8,128)} %bitcast.66, f32[256,128]{0,1:T(8,128)S(1)} %copy.23, ...), kind=kLoop, calls=%fused_computation.1 | loop fusion | flops 4186112 | bytes 8552448 | tf_op jit(solution)/shard_map/reduce_sum | solution.py:44
  60.5 1.1 %concatenate.3 = f32[64,128]{0,1:T(8,128)S(1)} concatenate(f32[8,128]{0,1:T(8,128)} %get-tuple-element.11, f32[8,128]{0,1:T(8,128)S(1)} %get-tuple-element.5, f32[8,128]{0,1:T(8,128)S(1)} %get-tuple-element.6, f32[8,128]{0,1:T(8,128)S(1)} %get-tuple-element.7, f32[8,128]{0,1:T(8,128)} %get-tuple-element.8, f32[8,128]{0,1:T(8,128)} %get-tuple-element.9, ...), dimensions={0} | concatenate | bytes 65536 | tf_op jit(solution)/shard_map/concatenate | solution.py:45
  61.7 36.4 %all-reduce = f32[64,128]{1,0:T(8,128)S(1)} all-reduce(f32[64,128]{1,0:T(8,128)S(1)} %copy.24), channel_id=3, replica_groups=mesh['row'=8,'col'=2,'rank'=2] {'row'}, use_global_device_ids=true, to_apply=%region_17.18.clone | all-reduce | flops 8192 | bytes 65536
  98.2 3.0 %psum.7 = f32[8,128]{1,0:T(8,128)} all-reduce(f32[8,128]{1,0:T(8,128)S(1)} %constant_dynamic-slice_fusion), channel_id=1, replica_groups=mesh['row'=8,'col'=2,'rank'=2] {'col'}, use_global_device_ids=true, to_apply=%region_18.19 | all-reduce | flops 1024 | bytes 8192 | tf_op jit(solution)/shard_map/psum | solution.py:60
  101.2 1.6 %copy.25 = f32[128,128]{1,0:T(8,128)} copy(f32[128,128]{0,1:T(8,128)} %reduce-scatter.2.cloned.1.call-done) | data formatting | bytes 131072
  (35 shorter events, 0.9 us)
Async XLA Ops:
  7.2 94.0 %reduce-scatter.2.cloned.1.call-start = ((), (), s32[]{:S(2)}) async-start(), calls=%async_computation.1 | async-start | bytes 196608 | tf_op jit(solution)/shard_map/reduce_scatter | solution.py:58
  7.2 5.1 %collective-permute-start = (bf16[1,128,128]{2,1,0:T(8,128)(2,1)}, bf16[1,128,128]{2,1,0:T(8,128)(2,1)S(1)}, u32[]{:S(2)}, u32[]{:S(2)}) collective-permute-start(bf16[1,128,128]{2,1,0:T(8,128)(2,1)} %bitcast.80), channel_id=1, source_target_pairs={{0,4},{4,0},{8,12},{12,8},{16,20},{20,16},{24,28},{28,24},{1,5},{5... | collective-permute-start | bytes 98312 | tf_op jit(solution)/shard_map/ppermute | solution.py:21
  13.1 4.4 %collective-permute-start.1 = (bf16[2,128,128]{2,1,0:T(8,128)(2,1)S(1)}, bf16[2,128,128]{2,1,0:T(8,128)(2,1)S(1)}, u32[]{:S(2)}, u32[]{:S(2)}) collective-permute-start(bf16[2,128,128]{2,1,0:T(8,128)(2,1)S(1)} %get-tuple-element.21), channel_id=1, source_target_pairs={{0,8},{4,12},{8,0},{12,4},{16,24},{20,28},{24,16},{28,20},{1,9},{5... | collective-permute-start | bytes 196616 | tf_op jit(solution)/shard_map/ppermute | solution.py:21
  17.6 9.1 %collective-permute-start.2 = (bf16[4,128,128]{2,1,0:T(8,128)(2,1)S(1)}, bf16[4,128,128]{2,1,0:T(8,128)(2,1)S(1)}, u32[]{:S(2)}, u32[]{:S(2)}) collective-permute-start(bf16[4,128,128]{2,1,0:T(8,128)(2,1)S(1)} %bitcast.76), channel_id=1, source_target_pairs={{0,16},{4,20},{8,24},{12,28},{16,0},{20,4},{24,8},{28,12},{1,17},{... | collective-permute-start | bytes 393224 | tf_op jit(solution)/shard_map/ppermute | solution.py:21
  26.8 25.9 %copy-start.6 = (f32[8,128]{0,1:T(8,128)S(1)}, f32[8,128]{0,1:T(8,128)}, u32[]{:S(2)}) copy-start(f32[8,128]{0,1:T(8,128)} %copy.15) | copy-start | bytes 12292
  26.8 25.9 %copy-start.8 = (f32[8,128]{0,1:T(8,128)S(1)}, f32[8,128]{0,1:T(8,128)}, u32[]{:S(2)}) copy-start(f32[8,128]{0,1:T(8,128)} %copy.16) | copy-start | bytes 12292
  26.8 26.6 %copy-start.7 = (f32[8,128]{0,1:T(8,128)S(1)}, f32[8,128]{0,1:T(8,128)}, u32[]{:S(2)}) copy-start(f32[8,128]{0,1:T(8,128)} %copy.18) | copy-start | bytes 12292
  26.8 27.9 %copy-start.5 = (f32[8,128]{0,1:T(8,128)S(1)}, f32[8,128]{0,1:T(8,128)}, u32[]{:S(2)}) copy-start(f32[8,128]{0,1:T(8,128)} %copy.22) | copy-start | bytes 12292
  51.3 2.1 %copy-start = (f32[16,8,8,256]{3,2,1,0:T(8,128)}, f32[16,8,8,256]{3,2,1,0:T(8,128)S(1)}, u32[]{:S(2)}) copy-start(f32[16,8,8,256]{3,2,1,0:T(8,128)S(1)} %copy.29) | copy-start | bytes 3145732
  51.6 2.5 %copy-start.1 = (f32[16,8,8,256]{3,2,1,0:T(8,128)}, f32[16,8,8,256]{3,2,1,0:T(8,128)S(1)}, u32[]{:S(2)}) copy-start(f32[16,8,8,256]{3,2,1,0:T(8,128)S(1)} %copy.30) | copy-start | bytes 3145732
  52.0 2.8 %copy-start.2 = (f32[16,8,8,256]{3,2,1,0:T(8,128)}, f32[16,8,8,256]{3,2,1,0:T(8,128)S(1)}, u32[]{:S(2)}) copy-start(f32[16,8,8,256]{3,2,1,0:T(8,128)S(1)} %copy.31) | copy-start | bytes 3145732
  52.3 3.1 %copy-start.3 = (f32[16,8,8,256]{3,2,1,0:T(8,128)}, f32[16,8,8,256]{3,2,1,0:T(8,128)S(1)}, u32[]{:S(2)}) copy-start(f32[16,8,8,256]{3,2,1,0:T(8,128)S(1)} %copy.32) | copy-start | bytes 3145732
  52.7 2.7 %copy-start.4 = (f32[16,8,8,256]{3,2,1,0:T(8,128)}, f32[16,8,8,256]{3,2,1,0:T(8,128)S(1)}, u32[]{:S(2)}) copy-start(f32[16,8,8,256]{3,2,1,0:T(8,128)S(1)} %copy.33) | copy-start | bytes 3145732
Sparse Core Ops, SparseCore 0:
  56.3 7.8 reduce-scatter.1
